TPU v7x, 32 devices: a whole 2x2x4 slice. The times are simulated.
32 devices in a mesh: rows: 8 (over y, x, core), snap: 4 (over z).
Axes of the slice: x: 2, y: 2, z: 4, core: 2. Of those that a mesh axis runs over, the one named last changes fastest.
Arguments:
- direct: bfloat16 [65536, 1024], P('rows', 'snap'), may hold values from -6 to 6
- adjoint: bfloat16 [65536, 1024], P('rows', 'snap'), may hold values from -6 to 6
- right_vectors: bfloat16 [1024, 256], replicated, may hold values from -0.1875 to 0.1875
- left_vectors: bfloat16 [1024, 256], replicated, may hold values from -0.1875 to 0.1875
- singular: float32 [256], replicated, may hold values from 0.25 to 4
Outputs:
- gram: float32 [1024, 1024], P('snap', 'rows')
- balancing: bfloat16 [65536, 256], P('rows', 'snap')
- adjoint_modes: bfloat16 [65536, 256], P('rows', 'snap')
All inputs are finite; a program needn't handle non-finite values.
Results may differ from a plain program's by a relative error of at most 0.0045.
Values may be sent and summed in bfloat16 or wider, within the bound.
A program may use at most 128 MiB of HBM per device.

v0:
```python
import jax
import jax.numpy as jnp
from jax import lax
from jax.sharding import PartitionSpec as P


def from_partner(block, axis, bit):
    count = lax.axis_size(axis)
    route = []
    for low in range(count):
        high = low | 1 << bit
        if high != low and high < count:
            route += [(low, high), (high, low)]
    return lax.ppermute(block, axis, route)


def on_device(direct, adjoint, right_vectors, left_vectors, singular):
    local_rows = direct.shape[0]
    block_cols = direct.shape[1]
    modes_all = right_vectors.shape[1]
    nsnap = lax.axis_size("snap")
    mode_cols = modes_all // nsnap
    snap_index = lax.axis_index("snap")
    nrows = local_rows * lax.axis_size("rows")
    mode_start = snap_index * mode_cols
    weights = lax.rsqrt(lax.dynamic_slice_in_dim(singular, mode_start, mode_cols, 0))
    nbits = nsnap.bit_length() - 1
    parity = snap_index % 2
    couple = snap_index // 2
    gathered = direct
    for level in range(1, nbits):
        other = from_partner(gathered, "snap", level)
        upper = snap_index // 2**level % 2
        gathered = jnp.where(
            upper == 1, jnp.concatenate([other, gathered], 1), jnp.concatenate([gathered, other], 1)
        )
    partner_y = from_partner(adjoint, "snap", 0)
    paired = jnp.where(
        parity == 1,
        jnp.concatenate([partner_y, adjoint], 1),
        jnp.concatenate([adjoint, partner_y], 1),
    )
    pair_gram = lax.dot_general(
        paired, gathered, (((0,), (0,)), ((), ())), preferred_element_type=jnp.float32
    )
    lower_rows = pair_gram[:block_cols]
    upper_rows = pair_gram[block_cols:]
    own_rows = jnp.where(parity == 1, upper_rows, lower_rows)
    send_rows = jnp.where(parity == 1, lower_rows, upper_rows)
    recv_rows = from_partner(send_rows.astype(jnp.bfloat16), "snap", 0).astype(send_rows.dtype)
    own_rows = own_rows.reshape(block_cols, nsnap // 2, block_cols)
    recv_rows = recv_rows.reshape(block_cols, nsnap // 2, block_cols)
    even_cols = jnp.where(parity == 0, own_rows, recv_rows)
    odd_cols = jnp.where(parity == 0, recv_rows, own_rows)
    partial_gram = jnp.stack([even_cols, odd_cols], 2).reshape(block_cols, block_cols * nsnap)
    pair_cols = lax.dynamic_slice_in_dim(right_vectors, couple * 2 * mode_cols, 2 * mode_cols, 1)
    pair_cols = pair_cols.reshape(nsnap // 2, 2, block_cols, 2 * mode_cols)
    chosen_v = lax.dynamic_index_in_dim(pair_cols, parity, 1, keepdims=False).reshape(
        -1, 2 * mode_cols
    )
    balance_part = jnp.dot(gathered, chosen_v, preferred_element_type=jnp.float32)
    first_half = balance_part[:, :mode_cols]
    second_half = balance_part[:, mode_cols:]
    own_part = jnp.where(parity == 1, second_half, first_half)
    send_part = jnp.where(parity == 1, first_half, second_half)
    balance_acc = own_part + from_partner(send_part, "snap", 0)
    pair_rows = lax.dynamic_slice_in_dim(left_vectors, couple * 2 * block_cols, 2 * block_cols, 0)
    pair_rows = pair_rows.reshape(2 * block_cols, nsnap // 2, 2, mode_cols)
    chosen_u = lax.dynamic_index_in_dim(pair_rows, parity, 2, keepdims=False).reshape(
        2 * block_cols, -1
    )
    terms = jnp.dot(paired, chosen_u, preferred_element_type=jnp.float32)
    for level in range(nbits - 1, 0, -1):
        half = terms.shape[1] // 2
        low_part = terms[:, :half]
        high_part = terms[:, half:]
        upper = snap_index // 2**level % 2
        keep_part = jnp.where(upper == 1, high_part, low_part)
        give_part = jnp.where(upper == 1, low_part, high_part)
        terms = keep_part + from_partner(give_part, "snap", level)
    gram = lax.psum_scatter(
        partial_gram / jnp.sqrt(jnp.float32(nrows)), "rows", scatter_dimension=1, tiled=True
    )
    balancing = (balance_acc * weights).astype(jnp.bfloat16)
    adjoint_modes = (terms * weights).astype(jnp.bfloat16)
    return (gram, balancing, adjoint_modes)


def solution(mesh):
    return jax.shard_map(
        on_device,
        mesh=mesh,
        in_specs=(P("rows", "snap"), P("rows", "snap"), P(), P(), P()),
        out_specs=(P("snap", "rows"), P("rows", "snap"), P("rows", "snap")),
        check_vma=False,
    )
```

profile of v0, /device:TPU:0, one launch (start us, length us, event | category | flops | bytes accessed | tf_op | source)
XLA Modules:
  0.0 358.5 jit_solution(5754782576088262875)
XLA Ops:
  7.2 3.1 collective-permute-start
  10.3 2.6 collective-permute-start.1
  13.0 0.1 copy.11
  13.1 1.0 constant_dynamic-slice_fusion.3
  14.1 176.9 %collective-permute-done = bf16[8192,256]{1,0:T(8,128)(2,1)} collective-permute-done((bf16[8192,256]{1,0:T(8,128)(2,1)}, bf16[8192,256]{1,0:T(8,128)(2,1)}, u32[]{:S(2)}, u32[]{:S(2)}) %collective-permute-start) | collective-permute-done | bytes 4194336 | tf_op jit(solution)/shard_map/ppermute | solution.py:14
  191.0 9.0 %fusion.2 = f32[8192,128]{0,1:T(8,128)S(1)} fusion(bf16[512,128]{0,1:T(8,128)(2,1)S(1)} %bitcast.13, bf16[8192,256]{1,0:T(8,128)(2,1)} %param.6, bf16[8192,256]{1,0:T(8,128)(2,1)} %collective-permute-done, pred[]{:T(512)S(6)} %eq.11), kind=kOutput, calls=%fused_computation.8 | convolution fusion | flops 1111490560 | bytes 12713985 | tf_op jit(solution)/shard_map/dot_general | solution.py:72
  200.1 1.9 copy-done.1
  202.0 1.5 slice_select_fusion
  203.5 0.7 collective-permute-start.4
  204.3 0.7 copy-done.3
  204.9 6.8 %fusion = f32[8192,128]{0,1:T(8,128)S(1)} fusion(bf16[512,128]{1,0:T(8,128)(2,1)S(1)} %bitcast.12, bf16[8192,256]{1,0:T(8,128)(2,1)S(1)} %copy-done.3, bf16[8192,256]{1,0:T(8,128)(2,1)} %collective-permute-done.1, pred[]{:T(512)S(6)} %eq.22), kind=kOutput, calls=%fused_computation.6 | convolution fusion | flops 1111490560 | bytes 12713985 | tf_op jit(solution)/shard_map/dot_general | solution.py:61
  211.7 2.0 copy-done.2
  213.7 1.6 slice_select_fusion.1
  215.3 1.8 collective-permute-start.3
  217.1 10.3 %fusion.1 = f32[512,512]{0,1:T(8,128)S(1)} fusion(bf16[8192,256]{1,0:T(8,128)(2,1)S(1)} %copy-done.3, bf16[8192,256]{1,0:T(8,128)(2,1)} %collective-permute-done.1, pred[]{:T(512)S(6)} %eq.22, bf16[8192,256]{1,0:T(8,128)(2,1)S(1)} %copy-done.4, bf16[8192,256]{1,0:T(8,128)(2,1)} %collective-permute-done, pred[]{:T(512)S(6)} %eq.11), kind=kOutput, calls=%fused_computation.7 | convolution fusion | flops 4370464768 | bytes 17825794 | tf_op jit(solution)/shard_map/dot_general | solution.py:43
  227.4 1.4 collective-permute-start.2
  228.9 0.1 dynamic-slice_rsqrt_fusion
  229.0 83.8 %collective-permute-done.2 = bf16[256,512]{0,1:T(8,128)(2,1)S(1)} collective-permute-done((bf16[256,512]{0,1:T(8,128)(2,1)S(1)}, bf16[256,512]{0,1:T(8,128)(2,1)S(1)}, u32[]{:S(2)}, u32[]{:S(2)}) %collective-permute-start.2) | collective-permute-done | bytes 262176 | tf_op jit(solution)/shard_map/ppermute | solution.py:14
  312.7 0.1 convert_select_fusion.1
  312.8 0.1 maximum_multiply_fusion
  312.9 0.6 copy.9
  313.6 1.9 div.23
  315.5 6.9 %multiply_convert_fusion = (bf16[8192,64]{0,1:T(8,128)(2,1)}, bf16[8192,64]{0,1:T(8,128)(2,1)}) fusion(f32[8192,64]{0,1:T(8,128)} %collective-permute-done.4, f32[8192,128]{0,1:T(8,128)} %copy-done.1, f32[64]{0:T(128)S(1)} %dynamic-slice_rsqrt_fusion, pred[]{:T(512)S(6)} %eq.22, f32[8192,64]{0,1:T(8,128)} %collective-permute-done.3, ...), kind=kLoop, calls=%fused_computation.2 | loop fusion | flops 4194304 | bytes 14680322 | tf_op jit(solution)/shard_map/convert_element_type | solution.py:85
  322.4 29.2 %reduce-scatter.2.cloned.1.call-done = f32[256,128]{1,0:T(8,128)} async-done(((f32[256,1024]{1,0:T(8,128)}), f32[256,128]{1,0:T(8,128)}) %reduce-scatter.2.cloned.1.call-update) | async-done | bytes 131088 | tf_op jit(solution)/shard_map/reduce_scatter | solution.py:81
  (18 shorter events, 0.2 us)
Async XLA Ops:
  7.2 5.8 %copy-start = (bf16[1024,256]{1,0:T(8,128)(2,1)S(1)}, bf16[1024,256]{1,0:T(8,128)(2,1)}, u32[]{:S(2)}) copy-start(bf16[1024,256]{1,0:T(8,128)(2,1)} %param.8) | copy-start | bytes 1572868
  7.2 344.4 %reduce-scatter.2.cloned.1.call-start = ((), (), s32[]{:S(2)}) async-start(), calls=%async_computation.1 | async-start | bytes 1179648 | tf_op jit(solution)/shard_map/reduce_scatter | solution.py:81
  7.2 183.8 %collective-permute-start = (bf16[8192,256]{1,0:T(8,128)(2,1)}, bf16[8192,256]{1,0:T(8,128)(2,1)}, u32[]{:S(2)}, u32[]{:S(2)}) collective-permute-start(bf16[8192,256]{1,0:T(8,128)(2,1)} %param.6), channel_id=1, source_target_pairs={{0,1},{1,0},{2,3},{3,2},{4,5},{5,4},{6,7},{7,6},{8,9},{9,8},{10,11... | collective-permute-start | bytes 12582920 | tf_op jit(solution)/shard_map/ppermute | solution.py:14
  10.3 193.9 %collective-permute-start.1 = (bf16[8192,256]{1,0:T(8,128)(2,1)}, bf16[8192,256]{1,0:T(8,128)(2,1)}, u32[]{:S(2)}, u32[]{:S(2)}) collective-permute-start(bf16[8192,256]{1,0:T(8,128)(2,1)} %param.5), channel_id=1, source_target_pairs={{0,2},{2,0},{1,3},{3,1},{4,6},{6,4},{5,7},{7,5},{8,10},{10,8},{9,1... | collective-permute-start | bytes 12582920 | tf_op jit(solution)/shard_map/ppermute | solution.py:14
  200.0 1.9 copy-start.1
  202.0 2.9 copy-start.3
  203.5 111.9 %collective-permute-start.4 = (f32[8192,64]{0,1:T(8,128)}, f32[8192,64]{0,1:T(8,128)}, u32[]{:S(2)}, u32[]{:S(2)}) collective-permute-start(f32[8192,64]{0,1:T(8,128)} %slice_select_fusion), channel_id=1, source_target_pairs={{0,2},{2,0},{1,3},{3,1},{4,6},{6,4},{5,7},{7,5},{8,10},{10,8},{9,1... | collective-permute-start | bytes 6291464 | tf_op jit(solution)/shard_map/ppermute | solution.py:14
  211.7 2.0 copy-start.2
  213.7 3.4 copy-start.4
  215.3 13.6 %copy-start.5 = (f32[256]{0:T(256)S(1)}, f32[256]{0:T(256)}, u32[]{:S(2)}) copy-start(f32[256]{0:T(256)} %param.9) | copy-start | bytes 3076
  215.3 100.2 %collective-permute-start.3 = (f32[8192,64]{0,1:T(8,128)}, f32[8192,64]{0,1:T(8,128)}, u32[]{:S(2)}, u32[]{:S(2)}) collective-permute-start(f32[8192,64]{0,1:T(8,128)} %slice_select_fusion.1), channel_id=1, source_target_pairs={{0,1},{1,0},{2,3},{3,2},{4,5},{5,4},{6,7},{7,6},{8,9},{9,8},{10,11... | collective-permute-start | bytes 6291464 | tf_op jit(solution)/shard_map/ppermute | solution.py:14
  227.4 85.3 %collective-permute-start.2 = (bf16[256,512]{0,1:T(8,128)(2,1)S(1)}, bf16[256,512]{0,1:T(8,128)(2,1)S(1)}, u32[]{:S(2)}, u32[]{:S(2)}) collective-permute-start(bf16[256,512]{0,1:T(8,128)(2,1)S(1)} %select_convert_fusion), channel_id=1, source_target_pairs={{0,1},{1,0},{2,3},{3,2},{4,5},{5,4},{6,7},{7,6},{8,9},{9,8},{10,11... | collective-permute-start | bytes 786440 | tf_op jit(solution)/shard_map/ppermute | solution.py:14
Sparse Core Ops, SparseCore 0:
  315.6 35.9 reduce-scatter.1
where the time goes:
time: 359 us; the launch traced here: 358 us
  waiting for transfers between devices  290 us (81%)
  matrix products  26.1 us (7%)
  between operations  14.2 us (4%)
  other arithmetic  10.2 us (3%)
  starting transfers between devices  9.73 us (3%)
  local copies, waits for them, and re-layouts  8.38 us (2%)
    ppermute x5, waiting for transfers between devices, from_partner(): return lax.ppermute(block, axis, route)  261 us
    reduce_scatter x1, waiting for transfers between devices, on_device(): lax.psum_scatter(partial_gram / jnp.sqrt(jnp.float32(nrows)), 'rows', sca...  29.2 us
    dot_general x1, matrix products, on_device(): lax.dot_general(paired, gathered, (((0,), (0,)), ((), ())), preferred_ele...  10.3 us
    ppermute x5, starting transfers between devices, from_partner(): return lax.ppermute(block, axis, route)  9.69 us
    dot_general x1, matrix products, on_device(): terms = jnp.dot(paired, chosen_u, preferred_element_type=jnp.float32)  9.04 us
  transfers between devices with their start and end apart: 6, of which 3 were waited for; matrix products, arithmetic and copies ran while one was open for 11% of the time, Pallas kernels for 0%

commit v1 on v0

v1 whole, which is shorter than its diff:
```python
import jax
import jax.numpy as jnp
from jax import lax
from jax.sharding import PartitionSpec as P

CHUNKS = 2


def shifted(block, level):
    count = lax.axis_size("snap")
    return lax.ppermute(block, "snap", [(k, k ^ (1 << level)) for k in range(count)])


def swapped_by(blocks, index):
    level = 0
    while (1 << level) < len(blocks):
        odd = (index >> level) % 2 == 1
        blocks = [jnp.where(odd, blocks[k ^ (1 << level)], blocks[k]) for k in range(len(blocks))]
        level += 1
    return blocks


def gram_dot(y, x):
    return lax.dot_general(y, x, (((0,), (0,)), ((), ())), preferred_element_type=jnp.float32)


def mode_dot(block, vectors):
    return lax.dot_general(vectors, block, (((0,), (1,)), ((), ())), preferred_element_type=jnp.float32)


def on_device(direct, adjoint, right_vectors, left_vectors, singular):
    local_rows, block_cols = direct.shape
    modes_all = right_vectors.shape[1]
    nsnap = lax.axis_size("snap")
    nrow_devices = lax.axis_size("rows")
    mode_cols = modes_all // nsnap
    me = lax.axis_index("snap")
    my_row = lax.axis_index("rows")
    nrows = local_rows * nrow_devices
    nbits = nsnap.bit_length() - 1
    weights = lax.rsqrt(lax.dynamic_slice_in_dim(singular, me * mode_cols, mode_cols, 0))[:, None]

    def vectors_block(vectors, row_block, mode_block):
        return lax.dynamic_slice(
            vectors, (row_block * block_cols, mode_block * mode_cols), (block_cols, mode_cols)
        )

    step = local_rows // CHUNKS
    y_own = [adjoint[c * step : (c + 1) * step] for c in range(CHUNKS)]
    x_all = [[direct[c * step : (c + 1) * step]] for c in range(CHUNKS)]
    y_oth = []
    for c in range(CHUNKS):
        y_oth.append(shifted(y_own[c], 0))
        for level in range(1, nbits):
            x_all[c] = x_all[c] + [shifted(b, level) for b in x_all[c]]

    terms = []
    parts = []
    tiles = {}
    for c in range(CHUNKS):
        terms.append(
            [
                mode_dot(y_own[c], vectors_block(left_vectors, me, me ^ (2 * e)))
                + mode_dot(y_oth[c], vectors_block(left_vectors, me ^ 1, me ^ (2 * e)))
                for e in range(nsnap // 2)
            ]
        )
        parts.append(
            [
                sum(
                    mode_dot(x_all[c][e], vectors_block(right_vectors, me ^ (2 * e), me ^ a))
                    for e in range(nsnap // 2)
                )
                for a in range(2)
            ]
        )
        for e in range(nsnap // 2):
            for a, y in enumerate((y_own[c], y_oth[c])):
                tile = gram_dot(y, x_all[c][e])
                tiles[e, a] = tile if c == 0 else tiles[e, a] + tile

    last = x_all[CHUNKS - 1][nsnap // 2 - 1]
    balancing = []
    adjoint_modes = []
    for c in range(CHUNKS):
        group = terms[c]
        for level in range(nbits - 1, 0, -1):
            half = len(group) // 2
            send = [t.astype(jnp.bfloat16) for t in group[half:]]
            *send, _ = lax.optimization_barrier((*send, last))
            group = [t + shifted(s, level).astype(jnp.float32) for t, s in zip(group[:half], send)]
        adjoint_modes.append((group[0] * weights).astype(jnp.bfloat16))
        send, _ = lax.optimization_barrier((parts[c][1].astype(jnp.bfloat16), last))
        total = parts[c][0] + shifted(send, 0).astype(jnp.float32)
        balancing.append((total * weights).astype(jnp.bfloat16))
    balancing = jnp.concatenate(balancing, 1).T
    adjoint_modes = jnp.concatenate(adjoint_modes, 1).T

    per_block = nrow_devices // nsnap
    width = block_cols // per_block
    pieces = swapped_by([tiles[e, a] for e in range(nsnap // 2) for a in range(2)], me)
    stacked = jnp.concatenate(
        [t[:, h * width : (h + 1) * width] for t in pieces for h in range(per_block)], 0
    )
    piece = lax.psum_scatter(stacked, "rows", scatter_dimension=0, tiled=True)
    piece = piece / jnp.sqrt(jnp.float32(nrows))
    route = []
    for r in range(nrow_devices):
        j = r // per_block
        target = (j ^ 1) * per_block + r % per_block
        for s in range(nsnap):
            if j % 2 != s % 2:
                route.append((r * nsnap + s, target * nsnap + (s ^ 1)))
    crossed = lax.ppermute(piece, ("rows", "snap"), route)
    gram = jnp.where((my_row // per_block) % 2 == me % 2, piece, crossed)
    return (gram, balancing, adjoint_modes)


def solution(mesh):
    return jax.shard_map(
        on_device,
        mesh=mesh,
        in_specs=(P("rows", "snap"), P("rows", "snap"), P(), P(), P()),
        out_specs=(P("snap", "rows"), P("rows", "snap"), P("rows", "snap")),
        check_vma=False,
    )
```

time: 359 us -> 285 us (0.79); the launches traced: 358 us -> 280 us
  waiting for transfers between devices: 290 us -> 175 us
  matrix products: 26.1 us -> 61 us
  other arithmetic: 10.2 us -> 3.75 us
  local copies, waits for them, and re-layouts: 8.38 us -> 14.2 us
    ppermute x5 -> x9, waiting for transfers between devices: 261 us -> 175 us  [the longest x8 175 us: shifted(): lax.ppermute(block, 'snap', [(k, k ^ 1 << level) for k in range(count)])]
    dot_general x3 -> x24, matrix products: 26.1 us -> 61 us  [the longest x16 42.5 us: mode_dot(): lax.dot_general(vectors, block, (((0,), (1,)), ((), ())), preferred_eleme...]
    reduce_scatter x1, waiting for transfers between devices: 29.2 us -> 0.01 us  [on_device(): piece = lax.psum_scatter(stacked, 'rows', scatter_dimension=0, tiled=True)]
    slice x0 -> x2, local copies, waits for them, and re-layouts: none -> 7.03 us  [the longest x1 4.7 us: on_device(): y_own = [adjoint[c * step:(c + 1) * step] for c in range(CHUNKS)]]
    convert_element_type x2 -> x0, other arithmetic: 6.95 us -> none  [the longest x1 6.9 us: on_device(): adjoint_modes = (terms * weights).astype(jnp.bfloat16)]
    ppermute x5 -> x9, starting transfers between devices: 9.69 us -> 11.9 us  [the longest x8 11.2 us: shifted(): lax.ppermute(block, 'snap', [(k, k ^ 1 << level) for k in range(count)])]
  transfers between devices with their start and end apart: 6 -> 10, of which waited for: 3 -> 7; matrix products, arithmetic and copies ran while one was open for 11% -> 21% of each run, Pallas kernels for 0% -> 0%
where the time goes in v1:
time: 285 us; the launch traced here: 280 us
  waiting for transfers between devices  175 us (61%)
  matrix products  61 us (21%)
  between operations  14.3 us (5%)
  local copies, waits for them, and re-layouts  14.2 us (5%)
  starting transfers between devices  11.9 us (4%)
  other arithmetic  3.75 us (1%)
    ppermute x8, waiting for transfers between devices, shifted(): lax.ppermute(block, 'snap', [(k, k ^ 1 << level) for k in range(count)])  175 us
    dot_general x16, matrix products, mode_dot(): lax.dot_general(vectors, block, (((0,), (1,)), ((), ())), preferred_eleme...  42.5 us
    dot_general x8, matrix products, gram_dot(): lax.dot_general(y, x, (((0,), (0,)), ((), ())), preferred_element_type=jn...  18.6 us
    ppermute x8, starting transfers between devices, shifted(): lax.ppermute(block, 'snap', [(k, k ^ 1 << level) for k in range(count)])  11.2 us
    unnamed x39, local copies, waits for them, and re-layouts  6.46 us
  transfers between devices with their start and end apart: 10, of which 7 were waited for; matrix products, arithmetic and copies ran while one was open for 21% of the time, Pallas kernels for 0%

profile of v1, /device:TPU:0, one launch (start us, length us, event | category | flops | bytes accessed | tf_op | source)
XLA Modules:
  0.0 280.0 jit_solution(4100205109883124057)
XLA Ops:
  7.2 4.7 %fusion.60 = (bf16[4096,256]{1,0:T(8,128)(2,1)}, bf16[4096,256]{1,0:T(8,128)(2,1)}) fusion(bf16[8192,256]{1,0:T(8,128)(2,1)} %param.6), kind=kLoop, calls=%fused_computation.93 | loop fusion | bytes 8388608 | tf_op jit(solution)/shard_map/slice | solution.py:49
  11.9 3.1 %collective-permute-start.2 = (bf16[4096,256]{1,0:T(8,128)(2,1)}, bf16[4096,256]{1,0:T(8,128)(2,1)S(1)}, u32[]{:S(2)}, u32[]{:S(2)}) collective-permute-start(bf16[4096,256]{1,0:T(8,128)(2,1)} %get-tuple-element.14), channel_id=1, source_target_pairs={{0,1},{1,0},{2,3},{3,2},{4,5},{5,4},{6,7},{7,6},{8,9},{9,8},{10,11... | collective-permute-start | bytes 6291464 | tf_op jit(solution)/shard_map/ppermute | solution.py:11
  17.3 2.6 collective-permute-start.3
  20.4 3.4 %fusion.36 = f32[64,4096]{1,0:T(8,128)} fusion(bf16[1024,256]{1,0:T(8,128)(2,1)S(1)} %copy-done, s32[]{:T(128)S(6)} %select_n.131, s32[]{:T(128)S(6)} %select_n.132, bf16[8192,256]{1,0:T(8,128)(2,1)} %param.5), kind=kOutput, calls=%fused_computation.68 | convolution fusion | flops 134217728 | bytes 3211272 | tf_op jit(solution)/shard_map/dot_general | solution.py:28
  23.8 3.4 %fusion.38 = f32[64,4096]{1,0:T(8,128)} fusion(bf16[1024,256]{1,0:T(8,128)(2,1)S(1)} %copy-done, s32[]{:T(128)S(6)} %select_n.131, s32[]{:T(128)S(6)} %select_n.132, bf16[8192,256]{1,0:T(8,128)(2,1)} %param.5), kind=kOutput, calls=%fused_computation.70 | convolution fusion | flops 134217728 | bytes 3211272 | tf_op jit(solution)/shard_map/dot_general | solution.py:28
  27.2 3.4 %fusion.30 = f32[64,4096]{1,0:T(8,128)} fusion(bf16[1024,256]{1,0:T(8,128)(2,1)S(1)} %copy-done, s32[]{:T(128)S(6)} %select_n.131, s32[]{:T(128)S(6)} %select_n.134, bf16[8192,256]{1,0:T(8,128)(2,1)} %param.5), kind=kOutput, calls=%fused_computation.62 | convolution fusion | flops 134217728 | bytes 3211272 | tf_op jit(solution)/shard_map/dot_general | solution.py:28
  30.6 3.5 %fusion.32 = f32[64,4096]{1,0:T(8,128)} fusion(bf16[1024,256]{1,0:T(8,128)(2,1)S(1)} %copy-done, s32[]{:T(128)S(6)} %select_n.131, s32[]{:T(128)S(6)} %select_n.134, bf16[8192,256]{1,0:T(8,128)(2,1)} %param.5), kind=kOutput, calls=%fused_computation.64 | convolution fusion | flops 134217728 | bytes 3211272 | tf_op jit(solution)/shard_map/dot_general | solution.py:28
  34.1 3.6 %fusion.24 = f32[64,4096]{1,0:T(8,128)} fusion(bf16[1024,256]{1,0:T(8,128)(2,1)S(1)} %copy-done.13, s32[]{:T(128)S(6)} %select_n.131, s32[]{:T(128)S(6)} %select_n.132, bf16[8192,256]{1,0:T(8,128)(2,1)} %param.6), kind=kOutput, calls=%fused_computation.56 | convolution fusion | flops 134217728 | bytes 3211272 | tf_op jit(solution)/shard_map/dot_general | solution.py:28
  37.7 3.4 %fusion.26 = f32[64,4096]{1,0:T(8,128)} fusion(bf16[1024,256]{1,0:T(8,128)(2,1)S(1)} %copy-done.13, s32[]{:T(128)S(6)} %select_n.131, s32[]{:T(128)S(6)} %select_n.132, bf16[8192,256]{1,0:T(8,128)(2,1)} %param.6), kind=kOutput, calls=%fused_computation.58 | convolution fusion | flops 134217728 | bytes 3211272 | tf_op jit(solution)/shard_map/dot_general | solution.py:28
  41.1 2.5 fusion.52
  47.7 3.0 %convolution_add_fusion.8 = f32[256,256]{1,0:T(8,128)S(1)} fusion(f32[256,256]{1,0:T(8,128)S(1)} %fusion.52, bf16[8192,256]{1,0:T(8,128)(2,1)} %param.5, bf16[8192,256]{1,0:T(8,128)(2,1)} %param.6), kind=kOutput, calls=%fused_computation.24 | convolution fusion | flops 536936448 | bytes 4718592 | tf_op jit(solution)/shard_map/dot_general | solution.py:24
  50.7 53.5 %collective-permute-done.2 = bf16[4096,256]{1,0:T(8,128)(2,1)S(1)} collective-permute-done((bf16[4096,256]{1,0:T(8,128)(2,1)}, bf16[4096,256]{1,0:T(8,128)(2,1)S(1)}, u32[]{:S(2)}, u32[]{:S(2)}) %collective-permute-start.2) | collective-permute-done | bytes 2097184 | tf_op jit(solution)/shard_map/ppermute | solution.py:11
  104.2 7.9 %collective-permute-done.3 = bf16[4096,256]{1,0:T(8,128)(2,1)} collective-permute-done((bf16[4096,256]{1,0:T(8,128)(2,1)}, bf16[4096,256]{1,0:T(8,128)(2,1)}, u32[]{:S(2)}, u32[]{:S(2)}) %collective-permute-start.3) | collective-permute-done | bytes 2097184 | tf_op jit(solution)/shard_map/ppermute | solution.py:11
  119.0 74.3 %collective-permute-done = bf16[4096,256]{1,0:T(8,128)(2,1)} collective-permute-done((bf16[4096,256]{1,0:T(8,128)(2,1)}, bf16[4096,256]{1,0:T(8,128)(2,1)}, u32[]{:S(2)}, u32[]{:S(2)}) %collective-permute-start) | collective-permute-done | bytes 2097184 | tf_op jit(solution)/shard_map/ppermute | solution.py:11
  195.7 4.9 %collective-permute-done.1 = bf16[4096,256]{1,0:T(8,128)(2,1)} collective-permute-done((bf16[4096,256]{1,0:T(8,128)(2,1)}, bf16[4096,256]{1,0:T(8,128)(2,1)}, u32[]{:S(2)}, u32[]{:S(2)}) %collective-permute-start.1) | collective-permute-done | bytes 2097184 | tf_op jit(solution)/shard_map/ppermute | solution.py:11
  200.5 3.0 %convolution_add_fusion.11 = f32[256,256]{1,0:T(8,128)S(1)} fusion(f32[256,256]{1,0:T(8,128)S(1)} %fusion.61, bf16[4096,256]{1,0:T(8,128)(2,1)} %collective-permute-done, bf16[4096,256]{1,0:T(8,128)(2,1)} %collective-permute-done.1), kind=kOutput, calls=%fused_computation.27 | convolution fusion | flops 536936448 | bytes 4718592 | tf_op jit(solution)/shard_map/dot_general | solution.py:24
  211.3 2.8 fusion.13
  214.1 2.5 fusion.12
  220.7 2.5 fusion.14
  225.1 21.3 %collective-permute-done.6 = bf16[64,4096]{1,0:T(8,128)(2,1)S(1)} collective-permute-done((bf16[64,4096]{1,0:T(8,128)(2,1)S(1)}, bf16[64,4096]{1,0:T(8,128)(2,1)S(1)}, u32[]{:S(2)}, u32[]{:S(2)}) %collective-permute-start.6) | collective-permute-done | bytes 524320 | tf_op jit(solution)/shard_map/ppermute | solution.py:11
  246.4 2.7 fusion.10
  249.0 6.3 %collective-permute-done.5 = bf16[64,4096]{1,0:T(8,128)(2,1)S(1)} collective-permute-done((bf16[64,4096]{1,0:T(8,128)(2,1)S(1)}, bf16[64,4096]{1,0:T(8,128)(2,1)S(1)}, u32[]{:S(2)}, u32[]{:S(2)}) %collective-permute-start.5) | collective-permute-done | bytes 524320 | tf_op jit(solution)/shard_map/ppermute | solution.py:11
  259.7 6.6 %collective-permute-done.7 = bf16[64,4096]{1,0:T(8,128)(2,1)S(1)} collective-permute-done((bf16[64,4096]{1,0:T(8,128)(2,1)S(1)}, bf16[64,4096]{1,0:T(8,128)(2,1)S(1)}, u32[]{:S(2)}, u32[]{:S(2)}) %collective-permute-start.7) | collective-permute-done | bytes 524320 | tf_op jit(solution)/shard_map/ppermute | solution.py:11
  266.2 2.5 fusion.9
  (68 shorter events, 38.5 us)
Async XLA Ops:
  7.2 13.2 %copy-start = (bf16[1024,256]{1,0:T(8,128)(2,1)S(1)}, bf16[1024,256]{1,0:T(8,128)(2,1)}, u32[]{:S(2)}) copy-start(bf16[1024,256]{1,0:T(8,128)(2,1)} %param.7) | copy-start | bytes 1572868
  7.2 262.6 %reduce-scatter.2.cloned.1.call-start = ((), (), s32[]{:S(2)}) async-start(), calls=%async_computation.1 | async-start | bytes 1179648 | tf_op jit(solution)/shard_map/reduce_scatter | solution.py:105
  7.2 7.8 %copy-start.1 = (bf16[8192,256]{1,0:T(8,128)(2,1)S(1)}, bf16[8192,256]{1,0:T(8,128)(2,1)}, u32[]{:S(2)}) copy-start(bf16[8192,256]{1,0:T(8,128)(2,1)} %param.5) | copy-start | bytes 12582916
  11.9 92.2 %collective-permute-start.2 = (bf16[4096,256]{1,0:T(8,128)(2,1)}, bf16[4096,256]{1,0:T(8,128)(2,1)S(1)}, u32[]{:S(2)}, u32[]{:S(2)}) collective-permute-start(bf16[4096,256]{1,0:T(8,128)(2,1)} %get-tuple-element.14), channel_id=1, source_target_pairs={{0,1},{1,0},{2,3},{3,2},{4,5},{5,4},{6,7},{7,6},{8,9},{9,8},{10,11... | collective-permute-start | bytes 6291464 | tf_op jit(solution)/shard_map/ppermute | solution.py:11
  17.3 94.8 %collective-permute-start.3 = (bf16[4096,256]{1,0:T(8,128)(2,1)}, bf16[4096,256]{1,0:T(8,128)(2,1)}, u32[]{:S(2)}, u32[]{:S(2)}) collective-permute-start(bf16[4096,256]{1,0:T(8,128)(2,1)} %get-tuple-element.12), channel_id=1, source_target_pairs={{0,2},{1,3},{2,0},{3,1},{4,6},{5,7},{6,4},{7,5},{8,10},{9,11},{10,... | collective-permute-start | bytes 6291464 | tf_op jit(solution)/shard_map/ppermute | solution.py:11
  19.9 173.4 %collective-permute-start = (bf16[4096,256]{1,0:T(8,128)(2,1)}, bf16[4096,256]{1,0:T(8,128)(2,1)}, u32[]{:S(2)}, u32[]{:S(2)}) collective-permute-start(bf16[4096,256]{1,0:T(8,128)(2,1)} %get-tuple-element.13), channel_id=1, source_target_pairs={{0,1},{1,0},{2,3},{3,2},{4,5},{5,4},{6,7},{7,6},{8,9},{9,8},{10,11... | collective-permute-start | bytes 6291464 | tf_op jit(solution)/shard_map/ppermute | solution.py:11
  20.4 180.2 %collective-permute-start.1 = (bf16[4096,256]{1,0:T(8,128)(2,1)}, bf16[4096,256]{1,0:T(8,128)(2,1)}, u32[]{:S(2)}, u32[]{:S(2)}) collective-permute-start(bf16[4096,256]{1,0:T(8,128)(2,1)} %get-tuple-element.11), channel_id=1, source_target_pairs={{0,2},{1,3},{2,0},{3,1},{4,6},{5,7},{6,4},{7,5},{8,10},{9,11},{10,... | collective-permute-start | bytes 6291464 | tf_op jit(solution)/shard_map/ppermute | solution.py:11
  30.6 3.5 %copy-start.13 = (bf16[1024,256]{1,0:T(8,128)(2,1)S(1)}, bf16[1024,256]{1,0:T(8,128)(2,1)}, u32[]{:S(2)}) copy-start(bf16[1024,256]{1,0:T(8,128)(2,1)} %param.8) | copy-start | bytes 1572868
  34.1 7.0 %copy-start.2 = (bf16[8192,256]{1,0:T(8,128)(2,1)S(1)}, bf16[8192,256]{1,0:T(8,128)(2,1)}, u32[]{:S(2)}) copy-start(bf16[8192,256]{1,0:T(8,128)(2,1)} %param.5) | copy-start | bytes 12582916
  41.1 2.8 %copy-start.4 = (bf16[8192,256]{1,0:T(8,128)(2,1)S(1)}, bf16[8192,256]{1,0:T(8,128)(2,1)}, u32[]{:S(2)}) copy-start(bf16[8192,256]{1,0:T(8,128)(2,1)} %param.6) | copy-start | bytes 12582916
  50.7 63.8 %copy-start.3 = (bf16[8192,256]{1,0:T(8,128)(2,1)S(1)}, bf16[8192,256]{1,0:T(8,128)(2,1)}, u32[]{:S(2)}) copy-start(bf16[8192,256]{1,0:T(8,128)(2,1)} %param.5) | copy-start | bytes 12582916
  211.2 2.9 %copy-start.10 = (f32[64,4096]{1,0:T(8,128)S(1)}, f32[64,4096]{1,0:T(8,128)}, u32[]{:S(2)}) copy-start(f32[64,4096]{1,0:T(8,128)} %fusion.32) | copy-start | bytes 3145732
  214.0 4.6 %copy-start.12 = (f32[64,4096]{1,0:T(8,128)S(1)}, f32[64,4096]{1,0:T(8,128)}, u32[]{:S(2)}) copy-start(f32[64,4096]{1,0:T(8,128)} %fusion.18) | copy-start | bytes 3145732
  214.1 32.3 %collective-permute-start.6 = (bf16[64,4096]{1,0:T(8,128)(2,1)S(1)}, bf16[64,4096]{1,0:T(8,128)(2,1)S(1)}, u32[]{:S(2)}, u32[]{:S(2)}) collective-permute-start(bf16[64,4096]{1,0:T(8,128)(2,1)S(1)} %fusion.13), channel_id=1, source_target_pairs={{0,1},{1,0},{2,3},{3,2},{4,5},{5,4},{6,7},{7,6},{8,9},{9,8},{10,11... | collective-permute-start | bytes 1572872 | tf_op jit(solution)/shard_map/ppermute | solution.py:11
  216.7 4.0 %copy-start.11 = (f32[64,4096]{1,0:T(8,128)S(1)}, f32[64,4096]{1,0:T(8,128)}, u32[]{:S(2)}) copy-start(f32[64,4096]{1,0:T(8,128)} %fusion.20) | copy-start | bytes 3145732
  216.7 38.7 %collective-permute-start.5 = (bf16[64,4096]{1,0:T(8,128)(2,1)S(1)}, bf16[64,4096]{1,0:T(8,128)(2,1)S(1)}, u32[]{:S(2)}, u32[]{:S(2)}) collective-permute-start(bf16[64,4096]{1,0:T(8,128)(2,1)S(1)} %fusion.12), channel_id=1, source_target_pairs={{0,1},{1,0},{2,3},{3,2},{4,5},{5,4},{6,7},{7,6},{8,9},{9,8},{10,11... | collective-permute-start | bytes 1572872 | tf_op jit(solution)/shard_map/ppermute | solution.py:11
  219.5 26.9 %copy-start.8 = (f32[64,4096]{1,0:T(8,128)S(1)}, f32[64,4096]{1,0:T(8,128)}, u32[]{:S(2)}) copy-start(f32[64,4096]{1,0:T(8,128)} %fusion.36) | copy-start | bytes 3145732
  219.5 38.3 %collective-permute-start.8 = (bf16[64,4096]{1,0:T(8,128)(2,1)S(1)}, bf16[64,4096]{1,0:T(8,128)(2,1)S(1)}, u32[]{:S(2)}, u32[]{:S(2)}) collective-permute-start(bf16[64,4096]{1,0:T(8,128)(2,1)S(1)} %fusion.15), channel_id=1, source_target_pairs={{0,2},{1,3},{2,0},{3,1},{4,6},{5,7},{6,4},{7,5},{8,10},{9,11},{10,... | collective-permute-start | bytes 1572872 | tf_op jit(solution)/shard_map/ppermute | solution.py:11
  223.2 32.2 %copy-start.7 = (f32[64,4096]{1,0:T(8,128)S(1)}, f32[64,4096]{1,0:T(8,128)}, u32[]{:S(2)}) copy-start(f32[64,4096]{1,0:T(8,128)} %fusion.38) | copy-start | bytes 3145732
  223.2 43.0 %collective-permute-start.7 = (bf16[64,4096]{1,0:T(8,128)(2,1)S(1)}, bf16[64,4096]{1,0:T(8,128)(2,1)S(1)}, u32[]{:S(2)}, u32[]{:S(2)}) collective-permute-start(bf16[64,4096]{1,0:T(8,128)(2,1)S(1)} %fusion.14), channel_id=1, source_target_pairs={{0,2},{1,3},{2,0},{3,1},{4,6},{5,7},{6,4},{7,5},{8,10},{9,11},{10,... | collective-permute-start | bytes 1572872 | tf_op jit(solution)/shard_map/ppermute | solution.py:11
  249.0 8.8 %copy-start.9 = (f32[64,4096]{1,0:T(8,128)S(1)}, f32[64,4096]{1,0:T(8,128)}, u32[]{:S(2)}) copy-start(f32[64,4096]{1,0:T(8,128)} %fusion.24) | copy-start | bytes 3145732
  257.9 8.4 %copy-start.6 = (f32[64,4096]{1,0:T(8,128)S(1)}, f32[64,4096]{1,0:T(8,128)}, u32[]{:S(2)}) copy-start(f32[64,4096]{1,0:T(8,128)} %fusion.26) | copy-start | bytes 3145732
  269.8 2.7 copy-start.14
  270.8 1.7 collective-permute-start.4
  (2 other events, 4.1 us)
Sparse Core Ops, SparseCore 0:
  211.4 36.0 reduce-scatter.1

commit v2 on v0

v2 whole, which is shorter than its diff:
```python
import functools
import math

import jax
import jax.numpy as jnp
from jax import lax
from jax.experimental import pallas as pl
from jax.experimental.pallas import tpu as pltpu
from jax.sharding import PartitionSpec as P

MESH = pl.DeviceIdType.MESH
CHUNKS = 8


def flipped(index, mask, bits):
    total = 0
    for b in range(bits):
        bit = (index // (1 << b)) % 2
        total = total + (1 << b) * ((1 - bit) if (mask >> b) & 1 else bit)
    return total


def kernel(
    nsnap, nrow, nchunks, root,
    x_hbm, y_hbm, vt, ut, weights, gram, balancing, adjoint_modes,
    x_own, y_own, x_oth, y_oth,
    bal_own, adj_own, bal_send, bal_recv, adj_send, adj_recv,
    acc, stage, slots, piece, crossed,
    local_sem, x_s, x_r, y_s, y_r, bal_s, bal_r, adj_s, adj_r, rs_s, rs_r, cross_s, cross_r,
):
    bits = nsnap.bit_length() - 1
    couples = nsnap // 2
    rows = x_own.shape[1]
    mode_cols = bal_own.shape[1]
    per_block = nrow // nsnap
    width = piece.shape[1]
    me = lax.axis_index("snap")
    row = lax.axis_index("rows")
    partner = flipped(me, 1, bits)
    far = [flipped(me, 2 * e, bits) for e in range(1, couples)]
    block = row // per_block
    opposite = row + per_block * (1 - 2 * (block % 2))
    outer = (me + me // 2) % 2 == 0
    crossing = (block + me) % 2 == 1

    def remote(src, dst, send, recv, target):
        return pltpu.make_async_remote_copy(
            src_ref=src, dst_ref=dst, send_sem=send, recv_sem=recv,
            device_id=target, device_id_type=MESH,
        )

    def x_copy(e, c):
        return remote(
            x_hbm.at[pl.ds(c * rows, rows)], x_oth.at[e, c], x_s.at[e, c], x_r.at[e, c], (row, far[e])
        )

    def y_copy(c):
        return remote(
            y_hbm.at[pl.ds(c * rows, rows)], y_oth.at[c], y_s.at[c], y_r.at[c], (row, partner)
        )

    def bal_copy(c):
        return remote(bal_send.at[c], bal_recv.at[c], bal_s.at[c], bal_r.at[c], (row, partner))

    def adj_copy(e, c):
        return remote(
            adj_send.at[e, c], adj_recv.at[e, c], adj_s.at[e, c], adj_r.at[e, c], (row, far[e])
        )

    def rs_copy(d):
        target = (row + d) % nrow
        return remote(stage.at[target], slots.at[d - 1], rs_s.at[d - 1], rs_r.at[d - 1], (target, me))

    def x_local(c):
        return pltpu.make_async_copy(x_hbm.at[pl.ds(c * rows, rows)], x_own.at[c], local_sem.at[0, c])

    def y_local(c):
        return pltpu.make_async_copy(y_hbm.at[pl.ds(c * rows, rows)], y_own.at[c], local_sem.at[1, c])

    def each(body):
        def step(c, carry):
            body(c)
            return carry

        lax.fori_loop(0, nchunks, step, 0)

    def each_far(make, act):
        def body(c):
            for e in range(couples - 1):
                act(make(e, c))

        each(body)

    start = lambda copy: copy.start()
    sent = lambda copy: copy.wait_send()

    barrier = pltpu.get_barrier_semaphore()
    peers = [(row, partner), (opposite, partner)] + [(row, f) for f in far]
    peers += [((row + d) % nrow, me) for d in range(1, nrow)]
    for peer in peers:
        pl.semaphore_signal(barrier, inc=1, device_id=peer, device_id_type=MESH)
    pl.semaphore_wait(barrier, len(peers))

    @pl.when(outer)
    def _():
        each(lambda c: start(y_copy(c)))
        each_far(x_copy, start)

    @pl.when(jnp.logical_not(outer))
    def _():
        each_far(x_copy, start)

    each(lambda c: (start(x_local(c)), start(y_local(c))))
    acc[...] = jnp.zeros_like(acc)

    @pl.when(jnp.logical_not(outer))
    def _():
        each_far(x_copy, sent)
        each(lambda c: start(y_copy(c)))

    def consume(c):
        x_local(c).wait()
        y_local(c).wait()
        y_copy(c).wait_recv()
        for e in range(couples - 1):
            x_copy(e, c).wait_recv()
        ys = (y_own.at[c], y_oth.at[c])
        xs = [x_own.at[c]] + [x_oth.at[e, c] for e in range(couples - 1)]
        for e in range(couples):
            for a in range(2):
                acc[2 * e + a] += lax.dot_general(
                    ys[a][...], xs[e][...], (((0,), (0,)), ((), ())), preferred_element_type=jnp.float32
                )
        nt = (((1,), (1,)), ((), ()))
        part = sum(
            lax.dot_general(vt[e], xs[e][...], nt, preferred_element_type=jnp.float32)
            for e in range(couples)
        )
        bal_own[c] = part[:mode_cols]
        bal_send[c] = part[mode_cols:].astype(jnp.bfloat16)
        term = sum(
            lax.dot_general(ut[a], ys[a][...], nt, preferred_element_type=jnp.float32) for a in range(2)
        )
        adj_own[c] = term[:mode_cols]
        for e in range(1, couples):
            adj_send[e - 1, c] = term[e * mode_cols : (e + 1) * mode_cols].astype(jnp.bfloat16)

    each(consume)

    for k in range(nsnap):
        target = flipped(me, k, bits) * per_block
        for h in range(per_block):
            stage[target + h] = acc[k, :, h * width : (h + 1) * width]
    for d in range(1, nrow):
        rs_copy(d).start()

    @pl.when(outer)
    def _():
        each(lambda c: start(bal_copy(c)))

    @pl.when(jnp.logical_not(outer))
    def _():
        each_far(adj_copy, start)

    total = stage[row]
    for d in range(1, nrow):
        rs_copy(d).wait_recv()
        total = total + slots[d - 1]
    piece[...] = total / jnp.float32(root)
    cross = remote(piece, crossed, cross_s, cross_r, (opposite, partner))

    @pl.when(crossing)
    def _():
        cross.start()

    @pl.when(outer)
    def _():
        each_far(adj_copy, start)
        each(lambda c: sent(y_copy(c)))
        each_far(x_copy, sent)
        each(lambda c: sent(bal_copy(c)))

    @pl.when(jnp.logical_not(outer))
    def _():
        each(lambda c: sent(y_copy(c)))
        each_far(adj_copy, sent)
        each(lambda c: start(bal_copy(c)))

    scale = weights[...]

    def finish(c):
        bal_copy(c).wait_recv()
        span = pl.ds(pl.multiple_of(c * rows, rows), rows)
        balancing[:, span] = ((bal_own[c] + bal_recv[c].astype(jnp.float32)) * scale).astype(jnp.bfloat16)
        value = adj_own[c]
        for e in range(couples - 1):
            adj_copy(e, c).wait_recv()
            value = value + adj_recv[e, c].astype(jnp.float32)
        adjoint_modes[:, span] = (value * scale).astype(jnp.bfloat16)

    each(finish)

    @pl.when(crossing)
    def _():
        cross.wait()
        gram[...] = crossed[...]

    @pl.when(jnp.logical_not(crossing))
    def _():
        gram[...] = piece[...]

    @pl.when(outer)
    def _():
        each_far(adj_copy, sent)

    @pl.when(jnp.logical_not(outer))
    def _():
        each(lambda c: sent(bal_copy(c)))

    for d in range(1, nrow):
        rs_copy(d).wait_send()


def on_device(direct, adjoint, right_vectors, left_vectors, singular):
    local_rows, block_cols = direct.shape
    nsnap = lax.axis_size("snap")
    nrow = lax.axis_size("rows")
    couples = nsnap // 2
    mode_cols = right_vectors.shape[1] // nsnap
    me = lax.axis_index("snap")
    root = math.sqrt(local_rows * nrow)
    weights = lax.rsqrt(lax.dynamic_slice_in_dim(singular, me * mode_cols, mode_cols, 0))[:, None]

    def part(vectors, row_block, mode_block):
        return lax.dynamic_slice(
            vectors, (row_block * block_cols, mode_block * mode_cols), (block_cols, mode_cols)
        ).T

    vt = jnp.stack(
        [
            jnp.concatenate([part(right_vectors, me ^ (2 * e), me ^ a) for a in range(2)], 0)
            for e in range(couples)
        ]
    )
    ut = jnp.stack(
        [
            jnp.concatenate([part(left_vectors, me ^ a, me ^ (2 * e)) for e in range(couples)], 0)
            for a in range(2)
        ]
    )
    nchunks = CHUNKS
    rows = local_rows // nchunks
    width = block_cols * nsnap // nrow
    vmem = pl.BlockSpec(memory_space=pltpu.VMEM)
    hbm = pl.BlockSpec(memory_space=pl.ANY)
    bf16, f32, dma = jnp.bfloat16, jnp.float32, pltpu.SemaphoreType.DMA
    modes = (nchunks, mode_cols, rows)
    gram, balancing, adjoint_modes = pl.pallas_call(
        functools.partial(kernel, nsnap, nrow, nchunks, root),
        out_shape=(
            jax.ShapeDtypeStruct((block_cols, width), f32),
            jax.ShapeDtypeStruct((mode_cols, local_rows), bf16),
            jax.ShapeDtypeStruct((mode_cols, local_rows), bf16),
        ),
        in_specs=[hbm, hbm, vmem, vmem, vmem],
        out_specs=(vmem, vmem, vmem),
        scratch_shapes=[
            pltpu.VMEM((nchunks, rows, block_cols), bf16),
            pltpu.VMEM((nchunks, rows, block_cols), bf16),
            pltpu.VMEM((couples - 1, nchunks, rows, block_cols), bf16),
            pltpu.VMEM((nchunks, rows, block_cols), bf16),
            pltpu.VMEM(modes, f32),
            pltpu.VMEM(modes, f32),
            pltpu.VMEM(modes, bf16),
            pltpu.VMEM(modes, bf16),
            pltpu.VMEM((couples - 1,) + modes, bf16),
            pltpu.VMEM((couples - 1,) + modes, bf16),
            pltpu.VMEM((nsnap, block_cols, block_cols), f32),
            pltpu.VMEM((nrow, block_cols, width), f32),
            pltpu.VMEM((nrow - 1, block_cols, width), f32),
            pltpu.VMEM((block_cols, width), f32),
            pltpu.VMEM((block_cols, width), f32),
            dma((2, nchunks)),
            dma((couples - 1, nchunks)),
            dma((couples - 1, nchunks)),
            dma((nchunks,)),
            dma((nchunks,)),
            dma((nchunks,)),
            dma((nchunks,)),
            dma((couples - 1, nchunks)),
            dma((couples - 1, nchunks)),
            dma((nrow - 1,)),
            dma((nrow - 1,)),
            dma(()),
            dma(()),
        ],
        compiler_params=pltpu.CompilerParams(
            collective_id=0, has_side_effects=True, vmem_limit_bytes=60 * 1024 * 1024
        ),
    )(direct, adjoint, vt, ut, weights)

    return (gram, balancing.T, adjoint_modes.T)


def solution(mesh):
    return jax.shard_map(
        on_device,
        mesh=mesh,
        in_specs=(P("rows", "snap"), P("rows", "snap"), P(), P(), P()),
        out_specs=(P("snap", "rows"), P("rows", "snap"), P("rows", "snap")),
        check_vma=False,
    )
```

time: 359 us -> 264 us (0.74)
  waiting for transfers between devices: 290 us -> 0 us
  Pallas kernels: 0 us -> 252 us
  matrix products: 26.1 us -> 0 us
  between operations: 14.2 us -> 0.77 us
  starting transfers between devices: 9.73 us -> 0 us
  other arithmetic: 10.2 us -> 1.37 us
    ppermute x5 -> x0, waiting for transfers between devices: 261 us -> none  [from_partner(): return lax.ppermute(block, axis, route)]
    pallas_call x0 -> x1, Pallas kernels: none -> 252 us  [on_device(): pl.pallas_call(functools.partial(kernel, nsnap, nrow, nchunks, root), out...]
    reduce_scatter x1 -> x0, waiting for transfers between devices: 29.2 us -> none  [on_device(): lax.psum_scatter(partial_gram / jnp.sqrt(jnp.float32(nrows)), 'rows', sca...]
    dot_general x3 -> x0, matrix products: 26.1 us -> none  [the longest x1 10.3 us: on_device(): lax.dot_general(paired, gathered, (((0,), (0,)), ((), ())), preferred_ele...]
    ppermute x5 -> x0, starting transfers between devices: 9.69 us -> none  [from_partner(): return lax.ppermute(block, axis, route)]
    convert_element_type x2 -> x0, other arithmetic: 6.95 us -> none  [the longest x1 6.9 us: on_device(): adjoint_modes = (terms * weights).astype(jnp.bfloat16)]
  transfers between devices with their start and end apart: 6 -> 0, of which waited for: 3 -> 0; matrix products, arithmetic and copies ran while one was open for 11% -> 0% of each run, Pallas kernels for 0% -> 0%
where the time goes in v2:
time: 264 us; the launch traced here: 263 us
  Pallas kernels  252 us (95%)
  local copies, waits for them, and re-layouts  9.59 us (4%)
    pallas_call x1, Pallas kernels, on_device(): pl.pallas_call(functools.partial(kernel, nsnap, nrow, nchunks, root), out...  252 us
    unnamed x11, local copies, waits for them, and re-layouts  6.81 us

profile of v2, /device:TPU:0, one launch (start us, length us, event | category | flops | bytes accessed | tf_op | source)
XLA Modules:
  0.0 263.3 jit_solution(743065286045459648)
XLA Ops:
  0.7 0.8 rsqrt_bitcast_fusion
  1.4 0.7 copy.16.weights
  2.1 1.3 fusion
  3.5 0.1 copy.21
  3.5 0.1 copy.23
  3.6 0.1 copy.22
  3.8 0.1 copy.24
  3.9 0.7 pad_maximum_fusion.1.ut
  4.5 0.1 copy.20
  4.6 0.1 copy.18
  4.7 0.1 copy.19
  4.8 0.1 copy.17
  5.0 0.7 pad_maximum_fusion.vt
  5.6 251.6 %shard_map.76 = (f32[256,128]{1,0:T(8,128)}, bf16[64,8192]{1,0:T(8,128)(2,1)}, bf16[64,8192]{1,0:T(8,128)(2,1)}) custom-call(bf16[8192,256]{1,0:T(8,128)(2,1)} %x_hbm.1, bf16[8192,256]{1,0:T(8,128)(2,1)} %y_hbm.1, bf16[2,128,256]{2,1,0:T(8,128)(2,1)} %pad_maximum_fusion.vt, bf16[2,128,256]{2,1,0:T(8,128)(2,1)} %pad_maximum_fusion.1.ut, f32[64,1]{1,0:T(8,128)} %copy.16.weights), custom_call_target="tpu_custom_call" | custom-call | tf_op jit(solution)/shard_map/pallas_call | solution.py:258
  257.2 1.6 copy.28
  258.8 2.3 copy.29
  261.0 2.3 copy.30
  (4 shorter events, 0.0 us)

commit v3 on v2

--- a/solution.py
+++ b/solution.py
@@ -101,51 +101,119 @@
         pl.semaphore_signal(barrier, inc=1, device_id=peer, device_id_type=MESH)
     pl.semaphore_wait(barrier, len(peers))
 
-    @pl.when(outer)
-    def _():
-        each(lambda c: start(y_copy(c)))
-        each_far(x_copy, start)
-
-    @pl.when(jnp.logical_not(outer))
-    def _():
-        each_far(x_copy, start)
-
-    each(lambda c: (start(x_local(c)), start(y_local(c))))
-    acc[...] = jnp.zeros_like(acc)
-
-    @pl.when(jnp.logical_not(outer))
-    def _():
-        each_far(x_copy, sent)
-        each(lambda c: start(y_copy(c)))
-
-    def consume(c):
-        x_local(c).wait()
-        y_local(c).wait()
-        y_copy(c).wait_recv()
-        for e in range(couples - 1):
-            x_copy(e, c).wait_recv()
-        ys = (y_own.at[c], y_oth.at[c])
-        xs = [x_own.at[c]] + [x_oth.at[e, c] for e in range(couples - 1)]
-        for e in range(couples):
-            for a in range(2):
-                acc[2 * e + a] += lax.dot_general(
-                    ys[a][...], xs[e][...], (((0,), (0,)), ((), ())), preferred_element_type=jnp.float32
-                )
-        nt = (((1,), (1,)), ((), ()))
+    ys = lambda c: (y_own.at[c], y_oth.at[c])
+    xs = lambda c: [x_own.at[c]] + [x_oth.at[e, c] for e in range(couples - 1)]
+    nt = (((1,), (1,)), ((), ()))
+
+    def bal_part(c):
         part = sum(
-            lax.dot_general(vt[e], xs[e][...], nt, preferred_element_type=jnp.float32)
-            for e in range(couples)
+            lax.dot_general(vt[e], x[...], nt, preferred_element_type=jnp.float32)
+            for e, x in enumerate(xs(c))
         )
         bal_own[c] = part[:mode_cols]
         bal_send[c] = part[mode_cols:].astype(jnp.bfloat16)
+
+    def adj_part(c):
         term = sum(
-            lax.dot_general(ut[a], ys[a][...], nt, preferred_element_type=jnp.float32) for a in range(2)
+            lax.dot_general(ut[a], y[...], nt, preferred_element_type=jnp.float32)
+            for a, y in enumerate(ys(c))
         )
         adj_own[c] = term[:mode_cols]
         for e in range(1, couples):
             adj_send[e - 1, c] = term[e * mode_cols : (e + 1) * mode_cols].astype(jnp.bfloat16)
 
-    each(consume)
+    def gram_part(c):
+        for e, x in enumerate(xs(c)):
+            for a, y in enumerate(ys(c)):
+                acc[2 * e + a] += lax.dot_general(
+                    y[...], x[...], (((0,), (0,)), ((), ())), preferred_element_type=jnp.float32
+                )
+
+    def x_arrived(c):
+        x_local(c).wait()
+        for e in range(couples - 1):
+            x_copy(e, c).wait_recv()
+
+    def y_arrived(c):
+        y_local(c).wait()
+        y_copy(c).wait_recv()
+
+    def all_at_once():
+        each(lambda c: start(y_copy(c)))
+        each_far(x_copy, start)
+        each(lambda c: (start(x_local(c)), start(y_local(c))))
+        acc[...] = jnp.zeros_like(acc)
+
+        def body(c):
+            x_arrived(c)
+            y_arrived(c)
+            bal_part(c)
+            bal_copy(c).start()
+            adj_part(c)
+            for e in range(couples - 1):
+                adj_copy(e, c).start()
+            gram_part(c)
+
+        each(body)
+        each_far(x_copy, sent)
+        each_far(adj_copy, sent)
+
+    def in_turns():
+        @pl.when(outer)
+        def _():
+            each(lambda c: start(y_copy(c)))
+
+        @pl.when(jnp.logical_not(outer))
+        def _():
+            each_far(x_copy, start)
+
+        each(lambda c: (start(x_local(c)), start(y_local(c))))
+        acc[...] = jnp.zeros_like(acc)
+
+        @pl.when(outer)
+        def _():
+            def body(c):
+                x_arrived(c)
+                bal_part(c)
+                bal_copy(c).start()
+
+            each(body)
+            each_far(x_copy, start)
+
+            def later(c):
+                y_arrived(c)
+                adj_part(c)
+                for e in range(couples - 1):
+                    adj_copy(e, c).start()
+                gram_part(c)
+
+            each(later)
+
+        @pl.when(jnp.logical_not(outer))
+        def _():
+            def body(c):
+                y_arrived(c)
+                adj_part(c)
+                for e in range(couples - 1):
+                    adj_copy(e, c).start()
+
+            each(body)
+            each_far(x_copy, sent)
+            each_far(adj_copy, sent)
+            each(lambda c: start(y_copy(c)))
+
+            def later(c):
+                x_arrived(c)
+                bal_part(c)
+                bal_copy(c).start()
+                gram_part(c)
+
+            each(later)
+
+    if couples == 2:
+        in_turns()
+    else:
+        all_at_once()
 
     for k in range(nsnap):
         target = flipped(me, k, bits) * per_block
@@ -154,14 +222,6 @@
     for d in range(1, nrow):
         rs_copy(d).start()
 
-    @pl.when(outer)
-    def _():
-        each(lambda c: start(bal_copy(c)))
-
-    @pl.when(jnp.logical_not(outer))
-    def _():
-        each_far(adj_copy, start)
-
     total = stage[row]
     for d in range(1, nrow):
         rs_copy(d).wait_recv()
@@ -172,19 +232,6 @@
     @pl.when(crossing)
     def _():
         cross.start()
-
-    @pl.when(outer)
-    def _():
-        each_far(adj_copy, start)
-        each(lambda c: sent(y_copy(c)))
-        each_far(x_copy, sent)
-        each(lambda c: sent(bal_copy(c)))
-
-    @pl.when(jnp.logical_not(outer))
-    def _():
-        each(lambda c: sent(y_copy(c)))
-        each_far(adj_copy, sent)
-        each(lambda c: start(bal_copy(c)))
 
     scale = weights[...]
 
@@ -209,13 +256,15 @@
     def _():
         gram[...] = piece[...]
 
-    @pl.when(outer)
-    def _():
-        each_far(adj_copy, sent)
-
-    @pl.when(jnp.logical_not(outer))
-    def _():
-        each(lambda c: sent(bal_copy(c)))
+    each(lambda c: sent(y_copy(c)))
+    each(lambda c: sent(bal_copy(c)))
+
+    if couples == 2:
+
+        @pl.when(outer)
+        def _():
+            each_far(x_copy, sent)
+            each_far(adj_copy, sent)
 
     for d in range(1, nrow):
         rs_copy(d).wait_send()

time: 264 us -> 249 us (0.943)
  Pallas kernels: 252 us -> 237 us
    pallas_call x1, Pallas kernels: 252 us -> 237 us  [on_device(): pl.pallas_call(functools.partial(kernel, nsnap, nrow, nchunks, root), out...]
where the time goes in v3:
time: 249 us
  Pallas kernels  237 us (95%)
  local copies, waits for them, and re-layouts  9.59 us (4%)
    pallas_call x1, Pallas kernels, on_device(): pl.pallas_call(functools.partial(kernel, nsnap, nrow, nchunks, root), out...  237 us
    unnamed x11, local copies, waits for them, and re-layouts  6.81 us

profile of v3, /device:TPU:0, one launch (start us, length us, event | category | flops | bytes accessed | tf_op | source)
XLA Modules:
  0.0 248.6 jit_solution(8389028127157355476)
XLA Ops:
  0.7 0.8 rsqrt_bitcast_fusion
  1.4 0.7 copy.16.weights
  2.1 1.3 fusion
  3.5 0.1 copy.21
  3.5 0.1 copy.23
  3.6 0.1 copy.22
  3.8 0.1 copy.24
  3.9 0.7 pad_maximum_fusion.1.ut
  4.5 0.1 copy.20
  4.6 0.1 copy.18
  4.7 0.1 copy.19
  4.8 0.1 copy.17
  5.0 0.7 pad_maximum_fusion.vt
  5.6 236.9 %shard_map.76 = (f32[256,128]{1,0:T(8,128)}, bf16[64,8192]{1,0:T(8,128)(2,1)}, bf16[64,8192]{1,0:T(8,128)(2,1)}) custom-call(bf16[8192,256]{1,0:T(8,128)(2,1)} %x_hbm.1, bf16[8192,256]{1,0:T(8,128)(2,1)} %y_hbm.1, bf16[2,128,256]{2,1,0:T(8,128)(2,1)} %pad_maximum_fusion.vt, bf16[2,128,256]{2,1,0:T(8,128)(2,1)} %pad_maximum_fusion.1.ut, f32[64,1]{1,0:T(8,128)} %copy.16.weights), custom_call_target="tpu_custom_call" | custom-call | tf_op jit(solution)/shard_map/pallas_call | solution.py:307
  242.5 1.6 copy.28
  244.1 2.3 copy.29
  246.4 2.3 copy.30
  (4 shorter events, 0.0 us)

commit v4 on v3

--- a/solution.py
+++ b/solution.py
@@ -344,7 +344,7 @@
             dma(()),
         ],
         compiler_params=pltpu.CompilerParams(
-            collective_id=0, has_side_effects=True, vmem_limit_bytes=60 * 1024 * 1024
+            collective_id=0, has_side_effects=True, vmem_limit_bytes=36 * 1024 * 1024
         ),
     )(direct, adjoint, vt, ut, weights)
 

time: 249 us -> 246 us (0.988)
  Pallas kernels: 237 us -> 234 us
    pallas_call x1, Pallas kernels: 237 us -> 234 us  [on_device(): pl.pallas_call(functools.partial(kernel, nsnap, nrow, nchunks, root), out...]
    unnamed x11 -> x15, local copies, waits for them, and re-layouts: 6.81 us -> 7.69 us
where the time goes in v4:
time: 246 us; the launch traced here: 245 us
  Pallas kernels  234 us (95%)
  local copies, waits for them, and re-layouts  9.86 us (4%)
    pallas_call x1, Pallas kernels, on_device(): pl.pallas_call(functools.partial(kernel, nsnap, nrow, nchunks, root), out...  234 us
    unnamed x15, local copies, waits for them, and re-layouts  7.69 us

profile of v4, /device:TPU:0, one launch (start us, length us, event | category | flops | bytes accessed | tf_op | source)
XLA Modules:
  0.0 244.8 jit_solution(5038546779453256320)
XLA Ops:
  0.7 0.8 rsqrt_bitcast_fusion
  1.4 0.1 copy.16.weights
  1.5 1.3 fusion
  2.8 0.1 copy.21
  2.9 0.1 copy.23
  3.0 0.1 copy.22
  3.1 0.1 copy.24
  3.3 0.1 copy.20
  3.4 0.1 copy.18
  3.5 0.1 copy.19
  3.6 0.1 copy.17
  3.7 0.0 copy-start
  3.7 2.2 copy-done
  5.9 0.0 copy-start.1
  5.9 2.2 copy-done.1
  8.1 234.1 %shard_map.76 = (f32[256,128]{1,0:T(8,128)S(1)}, bf16[64,8192]{1,0:T(8,128)(2,1)S(1)}, bf16[64,8192]{1,0:T(8,128)(2,1)S(1)}) custom-call(bf16[8192,256]{1,0:T(8,128)(2,1)S(1)} %copy-done, bf16[8192,256]{1,0:T(8,128)(2,1)S(1)} %copy-done.1, bf16[2,128,256]{2,1,0:T(8,128)(2,1)S(1)} %pad_maximum_fusion.vt, bf16[2,128,256]{2,1,0:T(8,128)(2,1)S(1)} %pad_maximum_fusion.1.ut, ...), custom_call_target="tpu_custom_call" | custom-call | tf_op jit(solution)/shard_map/pallas_call | solution.py:307
  242.2 0.7 copy.28
  242.9 1.0 copy.29
  243.9 1.0 copy.30
  (6 shorter events, 0.1 us)
Async XLA Ops:
  3.7 2.2 copy-start
  5.9 2.2 copy-start.1
